TPU v7x, 32 devices: a whole 2x2x4 slice. The times are simulated.
32 devices in a mesh: sa: 8 (over z, y), sb: 4 (over x, core).
Axes of the slice: x: 2, y: 2, z: 4, core: 2. Of those that a mesh axis runs over, the one named last changes fastest.
Arguments:
- queries: bfloat16 [16384, 4096], P(('sa', 'sb')), may hold values from -6 to 6
- keys: bfloat16 [16384, 4096], P(('sa', 'sb')), may hold values from -0.5390625 to 0.5390625
- values: bfloat16 [16384, 2048], P(('sa', 'sb')), may hold values from -6 to 6
- level_weights: bfloat16 [16384, 15, 32], P(('sa', 'sb')), may hold values from 0.25 to 4
- out_gain: bfloat16 [2048], replicated, may hold values from 0.25 to 1.75
Outputs:
- mixed: bfloat16 [16384, 2048], P(('sa', 'sb'))
All inputs are finite; a program needn't handle non-finite values.
Results may differ from a plain program's by a relative error of at most 0.008.
Values sent between devices are 32-bit elements; how exact they have to be, the bound alone decides.
A program may use at most 192 MiB of HBM per device.

v0:
```python
import jax
import jax.numpy as jnp
from jax import lax
from jax.sharding import PartitionSpec as P

DK = 128
DV = 64
TOK_BITS = 9


epsilon = 1e-06


def swapped(value, axis, distance):
    mask = 2**distance
    pairs = [(source, source ^ mask) for source in range(lax.axis_size(axis))]
    return lax.ppermute(value, axis, pairs)


def from_behind(block, axis, distance):
    devices = range(lax.axis_size(axis))
    route = [(i - distance, i) for i in devices if i - distance in devices]
    return lax.ppermute(block, axis, route)


def block_levels(length):
    position = jnp.arange(length, dtype=jnp.int32)
    xored = jnp.bitwise_xor(position[:, None], position[None, :])
    level_index = jnp.zeros((length, length), jnp.int32)
    for level_bit in range(TOK_BITS):
        level_index = level_index + (xored >= 1 << level_bit).astype(jnp.int32)
    causal = position[:, None] >= position[None, :]
    return (level_index, causal)


def pair_weights(level_index, causal, weight_rows):
    table = jnp.transpose(weight_rows[:, : TOK_BITS + 1, :].astype(jnp.float32), (2, 0, 1))
    weight = jnp.zeros((table.shape[0], level_index.shape[0], level_index.shape[1]), jnp.float32)
    for level_number in range(TOK_BITS + 1):
        weight = jnp.where(
            level_index[None] == level_number, table[:, :, level_number][:, :, None], weight
        )
    return jnp.where(causal[None], weight, 0.0)


def on_device(queries, keys, values, level_weights, out_gain):
    length = queries.shape[0]
    head_count = out_gain.shape[0] // DV
    query_matrix_rows = queries.reshape(length, head_count, DK)
    key_matrix_rows = keys.reshape(length, head_count, DK)
    value_matrix_rows = values.reshape(length, head_count, DV)
    level_index, causal = block_levels(length)
    weight = pair_weights(level_index, causal, level_weights)
    scores = jnp.einsum(
        "thk,shk->hts", query_matrix_rows, key_matrix_rows, preferred_element_type=jnp.float32
    )
    weighted = (scores * weight).astype(jnp.bfloat16)
    summed = jnp.einsum(
        "hts,shv->thv", weighted, value_matrix_rows, preferred_element_type=jnp.float32
    )
    segment_block_state = jnp.einsum(
        "tdw,tdr->dwr", key_matrix_rows, value_matrix_rows, preferred_element_type=jnp.float32
    )
    inner_size = lax.axis_size("sb")
    inner_bits = inner_size.bit_length() - 1
    outer_bits = lax.axis_size("sa").bit_length() - 1
    inner_index = lax.axis_index("sb")
    outer_index = lax.axis_index("sa")
    block_index = outer_index * inner_size + inner_index
    level_states = []
    carried = segment_block_state
    for rank_bit in range(inner_bits):
        partner = swapped(carried, "sb", rank_bit)
        level_states.append(partner)
        carried = carried + partner
    for rank_bit in range(outer_bits - 1):
        partner = swapped(carried, "sa", rank_bit)
        level_states.append(partner)
        carried = carried + partner
    top_bit = outer_bits - 1
    level_states.append(from_behind(carried, "sa", 1 << top_bit))
    for rank_bit, fenwick_level_state in enumerate(level_states):
        active_flag = (block_index >> rank_bit & 1).astype(jnp.float32)
        upper_half_state = fenwick_level_state.astype(jnp.bfloat16)
        lower_half_state = (fenwick_level_state - upper_half_state.astype(jnp.float32)).astype(
            jnp.bfloat16
        )
        state_readout_output = jnp.einsum(
            "jeu,eud->jed", query_matrix_rows, upper_half_state, preferred_element_type=jnp.float32
        )
        state_readout_output = state_readout_output + jnp.einsum(
            "jeu,eud->jed", query_matrix_rows, lower_half_state, preferred_element_type=jnp.float32
        )
        factor = level_weights[:, TOK_BITS + 1 + rank_bit, :].astype(jnp.float32) * active_flag
        summed = summed + factor[:, :, None] * state_readout_output
    inverse_rms = lax.rsqrt(jnp.mean(summed * summed, axis=-1, keepdims=True) + epsilon)
    gain_rows = out_gain.reshape(head_count, DV).astype(jnp.float32)
    return (summed * inverse_rms * gain_rows).reshape(length, head_count * DV).astype(jnp.bfloat16)


def solution(mesh):
    return jax.shard_map(
        on_device,
        mesh=mesh,
        in_specs=(
            P(("sa", "sb"), None),
            P(("sa", "sb"), None),
            P(("sa", "sb"), None),
            P(("sa", "sb"), None, None),
            P(),
        ),
        out_specs=P(("sa", "sb"), None),
        check_vma=False,
    )
```

profile of v0, /device:TPU:25, one launch (start us, length us, event | category | flops | bytes accessed | tf_op | source)
XLA Modules:
  0.0 197.7 jit_solution(2213836852873036816)
XLA Ops:
  0.0 2.9 %copy.20 = bf16[512,2048]{0,1:T(8,128)(2,1)S(1)} copy(bf16[512,2048]{1,0:T(8,128)(2,1)} %param.7) | data formatting | bytes 4194304 | tf_op args[2]
  2.9 0.0 copy-start.3
  2.9 0.0 copy-start.2
  2.9 4.2 %fusion.5 = f32[32,128,64]{1,2,0:T(8,128)} fusion(bf16[512,32,64]{0,2,1:T(8,128)(2,1)S(1)} %bitcast.157, bf16[512,4096]{1,0:T(8,128)(2,1)} %param.6), kind=kOutput, calls=%fused_computation.4 | convolution fusion | flops 268435456 | bytes 7340032 | tf_op jit(solution)/shard_map/tdw,tdr->dwr/dot_general | solution.py:61
  7.0 0.0 copy-start
  7.0 0.7 collective-permute-start
  7.7 0.3 iota_compare_fusion
  8.0 0.3 broadcast_compare_fusion.1
  8.4 0.3 broadcast_compare_fusion.3
  8.7 0.3 broadcast_compare_fusion.5
  9.1 0.3 broadcast_compare_fusion.7
  9.4 0.3 broadcast_compare_fusion.9
  9.7 0.0 copy-done.3
  9.7 0.1 convert_bitcast_fusion
  9.8 0.0 copy-done.2
  9.8 0.0 copy-done
  9.8 0.0 copy-start.4
  9.9 36.4 %multiply_convert_fusion.5 = bf16[32,512,512]{2,1,0:T(8,128)(2,1)} fusion(f32[32,512]{1,0:T(8,128)S(1)} %get-tuple-element.6, f32[32,512]{1,0:T(8,128)S(1)} %get-tuple-element.7, f32[32,512]{1,0:T(8,128)S(1)} %get-tuple-element.8, f32[32,512]{1,0:T(8,128)S(1)} %get-tuple-element.9, f32[32,512]{1,0:T(8,128)S(1)} %get-tuple-element.10, ...), kind=kOutput, calls=%fused_computation.clone.clone.1 | convolution fusion | flops 2256535552 | bytes 28704768 | tf_op jit(solution)/shard_map/thk,shk->hts/dot_general | solution.py:54
  46.3 0.0 copy-done.4
  46.3 0.1 reshape.226
  46.4 0.0 collective-permute-done
  46.4 1.4 add.499
  47.7 1.3 collective-permute-start.1
  49.0 10.7 %fusion = f32[32,512,64]{1,2,0:T(8,128)} fusion(bf16[512,32,64]{0,2,1:T(8,128)(2,1)S(1)} %bitcast.158, bf16[32,512,512]{2,1,0:T(8,128)(2,1)} %multiply_convert_fusion.5), kind=kOutput, calls=%fused_computation.1 | convolution fusion | flops 1073741824 | bytes 23068672 | tf_op jit(solution)/shard_map/hts,shv->thv/dot_general | solution.py:58
  59.7 12.8 %collective-permute-done.1 = f32[32,128,64]{1,2,0:T(8,128)S(1)} collective-permute-done((f32[32,128,64]{1,2,0:T(8,128)S(1)}, f32[32,128,64]{1,2,0:T(8,128)S(1)}, u32[]{:S(2)}, u32[]{:S(2)}) %collective-permute-start.1) | collective-permute-done | bytes 1048608 | tf_op jit(solution)/shard_map/ppermute | solution.py:17
  72.5 0.2 add.503
  72.7 1.3 collective-permute-start.2
  74.0 0.9 multiply_bitcast_fusion.4
  74.8 0.0 copy-done.1
  74.8 3.7 %fusion.23 = f32[32,64,512]{2,1,0:T(8,128)} fusion(f32[32,128,64]{1,2,0:T(8,128)S(1)} %collective-permute-done, bf16[512,4096]{1,0:T(8,128)(2,1)S(1)} %copy-done.1), kind=kOutput, calls=%fused_computation.22 | convolution fusion | flops 269484032 | bytes 9437184 | tf_op jit(solution)/shard_map/jeu,eud->jed/dot_general | solution.py:91
  78.5 3.5 %fusion.27 = f32[32,64,512]{2,1,0:T(8,128)} fusion(f32[32,128,64]{1,2,0:T(8,128)S(1)} %collective-permute-done, bf16[512,4096]{1,0:T(8,128)(2,1)S(1)} %copy-done.1), kind=kOutput, calls=%fused_computation.25 | convolution fusion | flops 268697600 | bytes 9437184 | tf_op jit(solution)/shard_map/jeu,eud->jed/dot_general | solution.py:88
  82.0 14.6 %collective-permute-done.2 = f32[32,128,64]{1,2,0:T(8,128)S(1)} collective-permute-done((f32[32,128,64]{1,2,0:T(8,128)S(1)}, f32[32,128,64]{1,2,0:T(8,128)S(1)}, u32[]{:S(2)}, u32[]{:S(2)}) %collective-permute-start.2) | collective-permute-done | bytes 1048608 | tf_op jit(solution)/shard_map/ppermute | solution.py:17
  96.6 0.1 add.507
  96.7 0.2 collective-permute-start.3
  97.0 3.5 %fusion.19 = f32[32,64,512]{2,1,0:T(8,128)} fusion(f32[32,128,64]{1,2,0:T(8,128)S(1)} %collective-permute-done.1, bf16[512,4096]{1,0:T(8,128)(2,1)S(1)} %copy-done.1), kind=kOutput, calls=%fused_computation.18 | convolution fusion | flops 269484032 | bytes 9437184 | tf_op jit(solution)/shard_map/jeu,eud->jed/dot_general | solution.py:91
  100.5 3.5 %fusion.21 = f32[32,64,512]{2,1,0:T(8,128)} fusion(f32[32,128,64]{1,2,0:T(8,128)S(1)} %collective-permute-done.1, bf16[512,4096]{1,0:T(8,128)(2,1)S(1)} %copy-done.1), kind=kOutput, calls=%fused_computation.20 | convolution fusion | flops 268697600 | bytes 9437184 | tf_op jit(solution)/shard_map/jeu,eud->jed/dot_general | solution.py:88
  104.0 3.5 %fusion.15 = f32[32,64,512]{2,1,0:T(8,128)} fusion(f32[32,128,64]{1,2,0:T(8,128)S(1)} %collective-permute-done.2, bf16[512,4096]{1,0:T(8,128)(2,1)S(1)} %copy-done.1), kind=kOutput, calls=%fused_computation.14 | convolution fusion | flops 269484032 | bytes 9437184 | tf_op jit(solution)/shard_map/jeu,eud->jed/dot_general | solution.py:91
  107.5 12.2 %collective-permute-done.3 = f32[32,128,64]{1,2,0:T(8,128)S(1)} collective-permute-done((f32[32,128,64]{1,2,0:T(8,128)S(1)}, f32[32,128,64]{1,2,0:T(8,128)S(1)}, u32[]{:S(2)}, u32[]{:S(2)}) %collective-permute-start.3) | collective-permute-done | bytes 1048608 | tf_op jit(solution)/shard_map/ppermute | solution.py:17
  119.8 0.2 add.511
  120.0 1.3 collective-permute-start.4
  121.3 3.6 %fusion.17 = f32[32,64,512]{2,1,0:T(8,128)} fusion(f32[32,128,64]{1,2,0:T(8,128)S(1)} %collective-permute-done.2, bf16[512,4096]{1,0:T(8,128)(2,1)S(1)} %copy-done.1), kind=kOutput, calls=%fused_computation.16 | convolution fusion | flops 268697600 | bytes 9437184 | tf_op jit(solution)/shard_map/jeu,eud->jed/dot_general | solution.py:88
  124.8 3.6 %fusion.11 = f32[32,64,512]{2,1,0:T(8,128)} fusion(f32[32,128,64]{1,2,0:T(8,128)S(1)} %collective-permute-done.3, bf16[512,4096]{1,0:T(8,128)(2,1)S(1)} %copy-done.1), kind=kOutput, calls=%fused_computation.10 | convolution fusion | flops 269484032 | bytes 9437184 | tf_op jit(solution)/shard_map/jeu,eud->jed/dot_general | solution.py:91
  128.4 3.5 %fusion.13 = f32[32,64,512]{2,1,0:T(8,128)} fusion(f32[32,128,64]{1,2,0:T(8,128)S(1)} %collective-permute-done.3, bf16[512,4096]{1,0:T(8,128)(2,1)S(1)} %copy-done.1), kind=kOutput, calls=%fused_computation.12 | convolution fusion | flops 268697600 | bytes 9437184 | tf_op jit(solution)/shard_map/jeu,eud->jed/dot_general | solution.py:88
  131.9 38.3 %collective-permute-done.4 = f32[32,128,64]{1,2,0:T(8,128)S(1)} collective-permute-done((f32[32,128,64]{1,2,0:T(8,128)S(1)}, f32[32,128,64]{1,2,0:T(8,128)S(1)}, u32[]{:S(2)}, u32[]{:S(2)}) %collective-permute-start.4) | collective-permute-done | bytes 1048608 | tf_op jit(solution)/shard_map/ppermute | solution.py:23
  170.2 3.6 %fusion.7 = f32[32,64,512]{2,1,0:T(8,128)} fusion(f32[32,128,64]{1,2,0:T(8,128)S(1)} %collective-permute-done.4, bf16[512,4096]{1,0:T(8,128)(2,1)S(1)} %copy-done.1), kind=kOutput, calls=%fused_computation.6 | convolution fusion | flops 269484032 | bytes 9437184 | tf_op jit(solution)/shard_map/jeu,eud->jed/dot_general | solution.py:91
  173.8 18.8 %multiply_reduce_fusion = (f32[512,32]{0,1:T(8,128)S(1)}, f32[512,32,64]{0,2,1:T(8,128)}) fusion(f32[32,64,512]{2,1,0:T(8,128)} %fusion.7, f32[32,128,64]{1,2,0:T(8,128)S(1)} %collective-permute-done.4, f32[512,32]{0,1:T(8,128)S(1)} %get-tuple-element.18, f32[32,64,512]{2,1,0:T(8,128)} %fusion.13, f32[32,64,512]{2,1,0:T(8,128)} %fusion.11, ...), kind=kOutput, calls=%fused_computation.38 | convolution fusion | flops 286507008 | bytes 51773440 | tf_op jit(solution)/shard_map/jeu,eud->jed/dot_general | solution.py:88
  192.6 2.7 %multiply_convert_fusion.2 = bf16[512,32,64]{0,2,1:T(8,128)(2,1)S(1)} fusion(f32[512,32,64]{0,2,1:T(8,128)} %get-tuple-element.21, f32[32,64]{1,0:T(8,128)S(1)} %reshape.226, f32[512,32]{0,1:T(8,128)S(1)} %add_rsqrt_fusion), kind=kLoop, calls=%fused_computation.37 | loop fusion | flops 3145728 | bytes 6365184 | tf_op jit(solution)/shard_map/convert_element_type | solution.py:98
  195.3 2.4 %copy.32 = bf16[512,2048]{1,0:T(8,128)(2,1)} copy(bf16[512,2048]{0,1:T(8,128)(2,1)S(1)} %bitcast.159) | data formatting | bytes 4194304 | tf_op jit(solution)/shard_map/convert_element_type | solution.py:98
  (3 shorter events, 0.1 us)
Async XLA Ops:
  2.9 6.8 %copy-start.3 = (bf16[512,15,32]{0,2,1:T(8,128)(2,1)S(1)}, bf16[512,15,32]{0,2,1:T(8,128)(2,1)}, u32[]{:S(2)}) copy-start(bf16[512,15,32]{0,2,1:T(8,128)(2,1)} %param.8) | copy-start | bytes 1474564
  2.9 7.0 %copy-start.2 = (bf16[512,4096]{1,0:T(8,128)(2,1)S(1)}, bf16[512,4096]{1,0:T(8,128)(2,1)}, u32[]{:S(2)}) copy-start(bf16[512,4096]{1,0:T(8,128)(2,1)} %param.6) | copy-start | bytes 12582916
  7.0 2.8 %copy-start = (bf16[512,4096]{1,0:T(8,128)(2,1)S(1)}, bf16[512,4096]{1,0:T(8,128)(2,1)}, u32[]{:S(2)}) copy-start(bf16[512,4096]{1,0:T(8,128)(2,1)} %param.5) | copy-start | bytes 12582916
  7.0 39.3 %collective-permute-start = (f32[32,128,64]{1,2,0:T(8,128)}, f32[32,128,64]{1,2,0:T(8,128)S(1)}, u32[]{:S(2)}, u32[]{:S(2)}) collective-permute-start(f32[32,128,64]{1,2,0:T(8,128)} %fusion.5), channel_id=1, source_target_pairs={{0,1},{1,0},{2,3},{3,2},{4,5},{5,4},{6,7},{7,6},{8,9},{9,8},{10,11... | collective-permute-start | bytes 3145736 | tf_op jit(solution)/shard_map/ppermute | solution.py:17
  9.8 36.4 %copy-start.4 = (bf16[2048]{0:T(1024)(128)(2,1)S(1)}, bf16[2048]{0:T(1024)(128)(2,1)}, u32[]{:S(2)}) copy-start(bf16[2048]{0:T(1024)(128)(2,1)} %param.9) | copy-start | bytes 12292
  47.7 24.8 %collective-permute-start.1 = (f32[32,128,64]{1,2,0:T(8,128)S(1)}, f32[32,128,64]{1,2,0:T(8,128)S(1)}, u32[]{:S(2)}, u32[]{:S(2)}) collective-permute-start(f32[32,128,64]{1,2,0:T(8,128)S(1)} %add.499), channel_id=1, source_target_pairs={{0,2},{1,3},{2,0},{3,1},{4,6},{5,7},{6,4},{7,5},{8,10},{9,11},{10,... | collective-permute-start | bytes 3145736 | tf_op jit(solution)/shard_map/ppermute | solution.py:17
  49.0 25.8 %copy-start.1 = (bf16[512,4096]{1,0:T(8,128)(2,1)S(1)}, bf16[512,4096]{1,0:T(8,128)(2,1)}, u32[]{:S(2)}) copy-start(bf16[512,4096]{1,0:T(8,128)(2,1)} %param.5) | copy-start | bytes 12582916
  72.7 23.9 %collective-permute-start.2 = (f32[32,128,64]{1,2,0:T(8,128)S(1)}, f32[32,128,64]{1,2,0:T(8,128)S(1)}, u32[]{:S(2)}, u32[]{:S(2)}) collective-permute-start(f32[32,128,64]{1,2,0:T(8,128)S(1)} %add.503), channel_id=1, source_target_pairs={{0,4},{4,0},{8,12},{12,8},{16,20},{20,16},{24,28},{28,24},{1,5},{5... | collective-permute-start | bytes 3145736 | tf_op jit(solution)/shard_map/ppermute | solution.py:17
  96.7 23.1 %collective-permute-start.3 = (f32[32,128,64]{1,2,0:T(8,128)S(1)}, f32[32,128,64]{1,2,0:T(8,128)S(1)}, u32[]{:S(2)}, u32[]{:S(2)}) collective-permute-start(f32[32,128,64]{1,2,0:T(8,128)S(1)} %add.507), channel_id=1, source_target_pairs={{0,8},{4,12},{8,0},{12,4},{16,24},{20,28},{24,16},{28,20},{1,9},{5... | collective-permute-start | bytes 3145736 | tf_op jit(solution)/shard_map/ppermute | solution.py:17
  120.0 50.3 %collective-permute-start.4 = (f32[32,128,64]{1,2,0:T(8,128)S(1)}, f32[32,128,64]{1,2,0:T(8,128)S(1)}, u32[]{:S(2)}, u32[]{:S(2)}) collective-permute-start(f32[32,128,64]{1,2,0:T(8,128)S(1)} %add.511), channel_id=1, source_target_pairs={{0,16},{4,20},{8,24},{12,28},{1,17},{5,21},{9,25},{13,29},{2,18},{... | collective-permute-start | bytes 3145736 | tf_op jit(solution)/shard_map/ppermute | solution.py:23
where the time goes:
time: 198 us
  matrix products  102 us (52%)
  waiting for transfers between devices  77.9 us (39%)
  other arithmetic  7.39 us (4%)
  local copies, waits for them, and re-layouts  5.38 us (3%)
  starting transfers between devices  4.79 us (2%)
    ppermute x4, waiting for transfers between devices, swapped(): return lax.ppermute(value, axis, pairs)  39.6 us
    ppermute x1, waiting for transfers between devices, from_behind(): return lax.ppermute(block, axis, route)  38.3 us
    dot_general x1, matrix products, on_device(): jnp.einsum('thk,shk->hts', query_matrix_rows, key_matrix_rows, preferred_...  36.4 us
    dot_general x5, matrix products, on_device(): jnp.einsum('jeu,eud->jed', query_matrix_rows, upper_half_state, preferred...  33 us
    dot_general x5, matrix products, on_device(): jnp.einsum('jeu,eud->jed', query_matrix_rows, lower_half_state, preferred...  17.8 us
    dot_general x1, matrix products, on_device(): jnp.einsum('hts,shv->thv', weighted, value_matrix_rows, preferred_element...  10.7 us
    dot_general x1, matrix products, on_device(): jnp.einsum('tdw,tdr->dwr', key_matrix_rows, value_matrix_rows, preferred_...  4.16 us
  transfers between devices with their start and end apart: 5, of which 4 were waited for; matrix products, arithmetic and copies ran while one was open for 40% of the time, Pallas kernels for 0%

commit v1 on v0

v1 whole, which is shorter than its diff:
```python
import functools

import jax
import jax.numpy as jnp
from jax import lax
from jax.experimental import pallas as pl
from jax.experimental.pallas import tpu as pltpu
from jax.sharding import PartitionSpec as P

DK = 128
DV = 64
TOK_BITS = 9
LANES = 128
TILE_BITS = 7
ROWS = 256
OWNED = 1

epsilon = 1e-06
MESH = pl.DeviceIdType.MESH
NT = (((1,), (1,)), ((), ()))
TN = (((0,), (0,)), ((), ()))


def lane_gather(value, index):
    return jnp.take_along_axis(value, index, axis=1, mode="promise_in_bounds")


def kernel(
    inner_bits, levels, chunks, slots, zero_slot,
    q_hbm, k_hbm, v_hbm, w_hbm, gain_ref, out_hbm,
    qb, kb, vb, wb, acc, ob, st, lvl, car, table,
    in_sem, out_sem, send_sem, recv_sem, pass_send, pass_recv,
):
    inner, outer = lax.axis_index("sb"), lax.axis_index("sa")
    length = qb.shape[1]
    pairs = 2 * OWNED
    core = inner % 2

    def bit(j):
        if j < inner_bits:
            return (inner // (1 << j)) % 2
        return (outer // (1 << (j - inner_bits))) % 2

    def partner(j):
        if j < inner_bits:
            return {"sb": inner + (1 << j) * (1 - 2 * bit(j))}
        return {"sa": outer + (1 << (j - inner_bits)) * (1 - 2 * bit(j))}

    def fetch(which, c):
        source, target, width = (
            (k_hbm, kb, 2 * pairs * DK), (v_hbm, vb, 2 * pairs * DV), (q_hbm, qb, 2 * pairs * DK)
        )[which]
        columns = pl.ds(pl.multiple_of(c * width, width), width)
        return pltpu.make_async_copy(source.at[:, columns], target.at[c], in_sem.at[which, c])

    weights_copy = pltpu.make_async_copy(w_hbm, wb, in_sem.at[3, 0])

    def put(c):
        width = pairs * 2 * DV
        columns = pl.ds(pl.multiple_of(c * width, width), width)
        return pltpu.make_async_copy(ob.at[c], out_hbm.at[:, columns], out_sem.at[c])

    mine = pl.ds(core * OWNED, OWNED)

    def exchange(j, c):
        if j == 0:
            source, target = st.at[c], lvl.at[0, c]
        else:
            source, target = car.at[j - 1, c], lvl.at[j, c, mine]
        return pltpu.make_async_remote_copy(
            src_ref=source, dst_ref=target, send_sem=send_sem.at[j, c],
            recv_sem=recv_sem.at[j, c], device_id=partner(j), device_id_type=MESH,
        )

    def pass_on(j, c):
        return pltpu.make_async_remote_copy(
            src_ref=lvl.at[j, c, mine], dst_ref=lvl.at[j, c, mine], send_sem=pass_send.at[j, c],
            recv_sem=pass_recv.at[j, c], device_id=partner(0), device_id_type=MESH,
        )

    for c in range(chunks):
        fetch(0, c).start()
        fetch(1, c).start()
        if c == 0:
            weights_copy.start()
            fetch(2, 0).start()
    for c in range(1, chunks):
        fetch(2, c).start()

    barrier = pltpu.get_barrier_semaphore()
    for j in range(levels):
        pl.semaphore_signal(barrier, inc=1, device_id=partner(j), device_id_type=MESH)

    row = lax.broadcasted_iota(jnp.int32, (LANES, LANES), 0)
    lane = lax.broadcasted_iota(jnp.int32, (LANES, LANES), 1)
    xored = jnp.bitwise_xor(row, lane)
    level = jnp.zeros((LANES, LANES), jnp.int32)
    for b in range(TILE_BITS):
        level = level + (xored >= (1 << b)).astype(jnp.int32)
    table[...] = jnp.where(row >= lane, level, zero_slot)
    pl.semaphore_wait(barrier, levels)

    def weight_place(c):
        start = c * (2 * pairs * slots)
        return start // LANES, start % LANES

    def block_states(c):
        for p in range(pairs):
            v = vb[c, :, p * 2 * DV : (p + 1) * 2 * DV]
            k = kb[c, :, p * 2 * DK : (p + 1) * 2 * DK]
            both = lax.dot_general(v, k, TN, preferred_element_type=jnp.float32)
            st[c, p, :DV, :] = both[:DV, :DK]
            st[c, p, DV:, :] = both[DV:, DK:]

    def local(c):
        group, offset = weight_place(c)
        for p in range(pairs):
            v = vb[c, :, p * 2 * DV : (p + 1) * 2 * DV]
            first = lax.broadcasted_iota(jnp.int32, v.shape, 1) < DV
            sides = (jnp.where(first, v, jnp.zeros_like(v)), jnp.where(first, jnp.zeros_like(v), v))
            for start in range(0, length, ROWS):
                total = None
                end = start + ROWS
                for side in range(2):
                    head = 2 * p + side
                    base = offset + head * slots
                    columns = slice(head * DK, (head + 1) * DK)
                    scores = lax.dot_general(
                        qb[c, start:end, columns], kb[c, :end, columns], NT,
                        preferred_element_type=jnp.float32,
                    )
                    strips = []
                    for t in range(start, end, LANES):
                        rows = wb[group, t : t + LANES, :]
                        strip, known = [], {}
                        for s in range(0, end, LANES):
                            if s > t:
                                strip.append(jnp.zeros((LANES, LANES), jnp.bfloat16))
                                continue
                            if s == t:
                                weight = lane_gather(rows, table[...] + base)
                            else:
                                number = (t ^ s).bit_length()
                                if number not in known:
                                    known[number] = lane_gather(
                                        rows, jnp.zeros((LANES, LANES), jnp.int32) + (base + number)
                                    )
                                weight = known[number]
                            piece = scores[t - start : t - start + LANES, s : s + LANES]
                            strip.append((piece * weight).astype(jnp.bfloat16))
                        strips.append(jnp.concatenate(strip, axis=1))
                    weighted = jnp.concatenate(strips, axis=0)
                    part = jnp.dot(weighted, sides[side][:end], preferred_element_type=jnp.float32)
                    total = part if total is None else total + part
                acc[c, start:end, p * LANES : (p + 1) * LANES] = total

    def finish(c):
        group, offset = weight_place(c)
        for p in range(pairs):
            states = []
            zero = jnp.zeros((DV, DK), jnp.bfloat16)
            for j in range(levels):
                state = jnp.where(bit(j) == 1, lvl[j, c, p], 0.0).astype(jnp.bfloat16)
                states.append(jnp.concatenate([state[:DV], zero], axis=1))
                states.append(jnp.concatenate([zero, state[DV:]], axis=1))
            for start in range(0, length, ROWS):
                q = qb[c, start : start + ROWS, p * 2 * DK : (p + 1) * 2 * DK]
                rows = wb[group, start : start + ROWS, :]
                right = (lax.broadcasted_iota(jnp.int32, (ROWS, LANES), 1) >= DV).astype(jnp.int32)
                place = right * slots + (offset + 2 * p * slots + TOK_BITS + 1)
                total = acc[c, start : start + ROWS, p * LANES : (p + 1) * LANES]
                for j in range(0, levels, 2):
                    stacked = jnp.concatenate(states[2 * j : 2 * j + 4], axis=0)
                    read = lax.dot_general(q, stacked, NT, preferred_element_type=jnp.float32)
                    for i in range(j, min(j + 2, levels)):
                        total = total + lane_gather(rows, place + i) * read[:, (i - j) * LANES : (i - j + 1) * LANES]
                square = total * total
                left = jnp.sum(jnp.where(right == 0, square, 0.0), axis=1, keepdims=True)
                other = jnp.sum(jnp.where(right == 0, 0.0, square), axis=1, keepdims=True)
                scale = jnp.where(
                    right == 0, lax.rsqrt(left * (1.0 / DV) + epsilon), lax.rsqrt(other * (1.0 / DV) + epsilon)
                )
                gain = gain_ref[c, :, p * LANES : (p + 1) * LANES]
                ob[c, start : start + ROWS, p * LANES : (p + 1) * LANES] = (total * scale * gain).astype(jnp.bfloat16)

    @pl.loop(0, chunks + levels + 1)
    def _(tick):
        @pl.when(tick < chunks)
        def _():
            fetch(0, tick).wait()
            fetch(1, tick).wait()
            block_states(tick)
            exchange(0, tick).start()

        for j in range(levels):
            c = tick - 1 - j

            @pl.when((c >= 0) & (c < chunks))
            def _(j=j, c=c):
                exchange(j, c).wait_recv()
                if j > 0:
                    pass_on(j, c).start()
                if j + 1 < levels:
                    own = st[c, mine] if j == 0 else car[j - 1, c]
                    car[j, c] = own + lvl[j, c, mine]
                    exchange(j + 1, c).start()

        @pl.when(tick == 0)
        def _():
            weights_copy.wait()

        @pl.when(tick < chunks)
        def _():
            fetch(2, tick).wait()
            local(tick)

        @pl.when(tick >= levels + 1)
        def _():
            c = tick - levels - 1
            for j in range(1, levels):
                pass_on(j, c).wait_recv()
            finish(c)
            put(c).start()

    @pl.loop(0, chunks)
    def _(c):
        put(c).wait()
        for j in range(levels):
            exchange(j, c).wait_send()
            if j > 0:
                pass_on(j, c).wait_send()


def on_device(queries, keys, values, level_weights, out_gain):
    length = queries.shape[0]
    heads = out_gain.shape[0] // DV
    count = level_weights.shape[1]
    inner_bits = lax.axis_size("sb").bit_length() - 1
    levels = inner_bits + lax.axis_size("sa").bit_length() - 1
    slots = 1 << count.bit_length()
    pairs = 2 * OWNED
    chunks = heads // (2 * pairs)
    weights = jnp.transpose(level_weights, (0, 2, 1))
    weights = jnp.pad(weights, ((0, 0), (0, 0), (0, slots - count)))
    weights = weights.reshape(length, heads * slots // LANES, LANES).astype(jnp.float32)
    weights = jnp.transpose(weights, (1, 0, 2))
    gain = out_gain.reshape(chunks, 1, pairs * 2 * DV).astype(jnp.float32)
    hbm = pl.BlockSpec(memory_space=pl.ANY)
    dma = pltpu.SemaphoreType.DMA
    return pl.pallas_call(
        functools.partial(kernel, inner_bits, levels, chunks, slots, count),
        out_shape=jax.ShapeDtypeStruct(values.shape, jnp.bfloat16),
        in_specs=[hbm, hbm, hbm, hbm, pl.BlockSpec(memory_space=pltpu.VMEM)],
        out_specs=hbm,
        scratch_shapes=[
            pltpu.VMEM((chunks, length, 2 * pairs * DK), jnp.bfloat16),
            pltpu.VMEM((chunks, length, 2 * pairs * DK), jnp.bfloat16),
            pltpu.VMEM((chunks, length, 2 * pairs * DV), jnp.bfloat16),
            pltpu.VMEM(weights.shape, jnp.float32),
            pltpu.VMEM((chunks, length, 2 * pairs * DV), jnp.float32),
            pltpu.VMEM((chunks, length, 2 * pairs * DV), jnp.bfloat16),
            pltpu.VMEM((chunks, pairs, 2 * DV, DK), jnp.float32),
            pltpu.VMEM((levels, chunks, pairs, 2 * DV, DK), jnp.float32),
            pltpu.VMEM((levels - 1, chunks, OWNED, 2 * DV, DK), jnp.float32),
            pltpu.VMEM((LANES, LANES), jnp.int32),
            dma((4, chunks)),
            dma((chunks,)),
            dma((levels, chunks)),
            dma((levels, chunks)),
            dma((levels, chunks)),
            dma((levels, chunks)),
        ],
        compiler_params=pltpu.CompilerParams(
            collective_id=0, has_side_effects=True, vmem_limit_bytes=56 * 1024 * 1024
        ),
    )(queries, keys, values, weights, gain)


def solution(mesh):
    return jax.shard_map(
        on_device,
        mesh=mesh,
        in_specs=(
            P(("sa", "sb"), None),
            P(("sa", "sb"), None),
            P(("sa", "sb"), None),
            P(("sa", "sb"), None, None),
            P(),
        ),
        out_specs=P(("sa", "sb"), None),
        check_vma=False,
    )
```

time: 198 us -> 61.6 us (0.31)
  the two profiles are of different devices: /device:TPU:25 before, /device:TPU:0 now
where the time goes in v1:
time: 61.6 us; the launch traced here: 61.3 us
  Pallas kernels  54 us (88%)
  local copies, waits for them, and re-layouts  5.83 us (9%)
  other arithmetic  1.4 us (2%)
    pallas_call x1, Pallas kernels, on_device(): pl.pallas_call(functools.partial(kernel, inner_bits, levels, chunks, slot...  54 us
    unnamed x2, local copies, waits for them, and re-layouts  4.46 us
    transpose x1, local copies, waits for them, and re-layouts, on_device(): weights = jnp.transpose(weights, (1, 0, 2))  1.31 us
    convert_element_type x1, other arithmetic, on_device(): gain = out_gain.reshape(chunks, 1, pairs * 2 * DV).astype(jnp.float32)  1.28 us

profile of v1, /device:TPU:0, one launch (start us, length us, event | category | flops | bytes accessed | tf_op | source)
XLA Modules:
  0.0 61.3 jit_solution(2868117155875892476)
XLA Ops:
  0.0 1.3 %convert_element_type.14 = f32[2048]{0:T(1024)} convert(bf16[2048]{0:T(1024)(128)(2,1)} %param.9) | non-fusion elementwise | flops 2048 | bytes 12288 | tf_op jit(solution)/shard_map/convert_element_type | solution.py:247
  1.3 1.3 %copy.9 = bf16[512,15,32]{0,1,2:T(8,128)(2,1)S(1)} copy(bf16[512,15,32]{0,2,1:T(8,128)(2,1)} %param.8) | data formatting | bytes 983040 | tf_op args[3]
  2.6 0.1 pad.4
  2.7 0.1 bitcast_convert_fusion
  2.8 1.3 %copy.7 = f32[512,4,128]{2,0,1:T(8,128)} copy(f32[512,4,128]{0,2,1:T(8,128)S(1)} %bitcast_convert_fusion) | data formatting | bytes 2097152 | tf_op jit(solution)/shard_map/transpose | solution.py:246
  4.1 54.0 %shard_map.55 = bf16[512,2048]{1,0:T(8,128)(2,1)} custom-call(bf16[512,4096]{1,0:T(8,128)(2,1)} %q_hbm.1, bf16[512,4096]{1,0:T(8,128)(2,1)} %k_hbm.1, bf16[512,2048]{1,0:T(8,128)(2,1)} %v_hbm.1, f32[4,512,128]{2,1,0:T(8,128)} %bitcast.9, f32[8,1,256]{2,1,0:T(1,128)} %bitcast.12), custom_call_target="tpu_custom_call" | custom-call | tf_op jit(solution)/shard_map/pallas_call | solution.py:250
  58.1 3.2 %copy.11 = bf16[512,2048]{1,0:T(8,128)(2,1)} copy(bf16[512,2048]{1,0:T(8,128)(2,1)} %shard_map.55) | data formatting | bytes 4194304

commit v2 on v1

--- a/solution.py
+++ b/solution.py
@@ -14,6 +14,10 @@
 TILE_BITS = 7
 ROWS = 256
 OWNED = 1
+NEAR = 3
+VMEM_MIB = 56
+NEAR_GAP = 2
+FAR_GAP = 2
 
 epsilon = 1e-06
 MESH = pl.DeviceIdType.MESH
@@ -26,9 +30,9 @@
 
 
 def kernel(
-    inner_bits, levels, chunks, slots, zero_slot,
-    q_hbm, k_hbm, v_hbm, w_hbm, gain_ref, out_hbm,
-    qb, kb, vb, wb, acc, ob, st, lvl, car, table,
+    inner_bits, levels, chunks, slots, zero_slot, heads,
+    q_hbm, k_hbm, v_hbm, w_hbm, out_hbm,
+    qb, kb, vb, wt, wb, acc, ob, st, lvl, car, table,
     in_sem, out_sem, send_sem, recv_sem, pass_send, pass_recv,
 ):
     inner, outer = lax.axis_index("sb"), lax.axis_index("sa")
@@ -53,7 +57,7 @@
         columns = pl.ds(pl.multiple_of(c * width, width), width)
         return pltpu.make_async_copy(source.at[:, columns], target.at[c], in_sem.at[which, c])
 
-    weights_copy = pltpu.make_async_copy(w_hbm, wb, in_sem.at[3, 0])
+    weights_copy = pltpu.make_async_copy(w_hbm, wt, in_sem.at[3, 0])
 
     def put(c):
         width = pairs * 2 * DV
@@ -103,6 +107,13 @@
     def weight_place(c):
         start = c * (2 * pairs * slots)
         return start // LANES, start % LANES
+
+    def spread_weights(group):
+        shape = (wt.shape[0], LANES)
+        slot = lax.broadcasted_iota(jnp.int32, shape, 1) + group * LANES
+        wanted = (slot & (slots - 1)) * heads + lax.shift_right_logical(slot, slots.bit_length() - 1)
+        chosen = (lax.broadcasted_iota(jnp.int32, shape, 0) == wanted).astype(jnp.bfloat16)
+        wb[group] = lax.dot_general(wt[...], chosen, TN, preferred_element_type=jnp.float32)
 
     def block_states(c):
         for p in range(pairs):
@@ -180,10 +191,14 @@
                 scale = jnp.where(
                     right == 0, lax.rsqrt(left * (1.0 / DV) + epsilon), lax.rsqrt(other * (1.0 / DV) + epsilon)
                 )
-                gain = gain_ref[c, :, p * LANES : (p + 1) * LANES]
-                ob[c, start : start + ROWS, p * LANES : (p + 1) * LANES] = (total * scale * gain).astype(jnp.bfloat16)
-
-    @pl.loop(0, chunks + levels + 1)
+                ob[c, start : start + ROWS, p * LANES : (p + 1) * LANES] = (total * scale).astype(jnp.bfloat16)
+
+    arrival = [1]
+    for j in range(1, levels):
+        arrival.append(arrival[-1] + (NEAR_GAP if j < NEAR else FAR_GAP))
+    last = arrival[-1] + 1
+
+    @pl.loop(0, chunks + last)
     def _(tick):
         @pl.when(tick < chunks)
         def _():
@@ -193,7 +208,7 @@
             exchange(0, tick).start()
 
         for j in range(levels):
-            c = tick - 1 - j
+            c = tick - arrival[j]
 
             @pl.when((c >= 0) & (c < chunks))
             def _(j=j, c=c):
@@ -212,11 +227,17 @@
         @pl.when(tick < chunks)
         def _():
             fetch(2, tick).wait()
+            group, offset = weight_place(tick)
+
+            @pl.when(offset == 0)
+            def _():
+                spread_weights(group)
+
             local(tick)
 
-        @pl.when(tick >= levels + 1)
+        @pl.when(tick >= last)
         def _():
-            c = tick - levels - 1
+            c = tick - last
             for j in range(1, levels):
                 pass_on(j, c).wait_recv()
             finish(c)
@@ -240,23 +261,20 @@
     slots = 1 << count.bit_length()
     pairs = 2 * OWNED
     chunks = heads // (2 * pairs)
-    weights = jnp.transpose(level_weights, (0, 2, 1))
-    weights = jnp.pad(weights, ((0, 0), (0, 0), (0, slots - count)))
-    weights = weights.reshape(length, heads * slots // LANES, LANES).astype(jnp.float32)
-    weights = jnp.transpose(weights, (1, 0, 2))
-    gain = out_gain.reshape(chunks, 1, pairs * 2 * DV).astype(jnp.float32)
-    hbm = pl.BlockSpec(memory_space=pl.ANY)
+    weights = jnp.transpose(level_weights, (1, 2, 0)).reshape(count * heads, length)
+    hbm = pl.BlockSpec(memory_space=pltpu.HBM)
     dma = pltpu.SemaphoreType.DMA
-    return pl.pallas_call(
-        functools.partial(kernel, inner_bits, levels, chunks, slots, count),
+    unit = pl.pallas_call(
+        functools.partial(kernel, inner_bits, levels, chunks, slots, count, heads),
         out_shape=jax.ShapeDtypeStruct(values.shape, jnp.bfloat16),
-        in_specs=[hbm, hbm, hbm, hbm, pl.BlockSpec(memory_space=pltpu.VMEM)],
-        out_specs=hbm,
+        in_specs=[hbm, hbm, hbm, hbm],
+        out_specs=pl.BlockSpec(memory_space=pl.ANY),
         scratch_shapes=[
             pltpu.VMEM((chunks, length, 2 * pairs * DK), jnp.bfloat16),
             pltpu.VMEM((chunks, length, 2 * pairs * DK), jnp.bfloat16),
             pltpu.VMEM((chunks, length, 2 * pairs * DV), jnp.bfloat16),
-            pltpu.VMEM(weights.shape, jnp.float32),
+            pltpu.VMEM(weights.shape, jnp.bfloat16),
+            pltpu.VMEM((heads * slots // LANES, length, LANES), jnp.float32),
             pltpu.VMEM((chunks, length, 2 * pairs * DV), jnp.float32),
             pltpu.VMEM((chunks, length, 2 * pairs * DV), jnp.bfloat16),
             pltpu.VMEM((chunks, pairs, 2 * DV, DK), jnp.float32),
@@ -271,9 +289,10 @@
             dma((levels, chunks)),
         ],
         compiler_params=pltpu.CompilerParams(
-            collective_id=0, has_side_effects=True, vmem_limit_bytes=56 * 1024 * 1024
+            collective_id=0, has_side_effects=True, vmem_limit_bytes=VMEM_MIB * 1024 * 1024
         ),
-    )(queries, keys, values, weights, gain)
+    )(queries, keys, values, weights)
+    return unit * out_gain
 
 
 def solution(mesh):

time: 61.6 us -> 53.6 us (0.87)
  local copies, waits for them, and re-layouts: 5.83 us -> 0.01 us
  Pallas kernels: 54 us -> 50.4 us
  other arithmetic: 1.4 us -> 3.05 us
    unnamed x2, local copies, waits for them, and re-layouts: 4.46 us -> 0.01 us
    pallas_call x1, Pallas kernels: 54 us -> 50.4 us  [on_device(): pl.pallas_call(functools.partial(kernel, inner_bits, levels, chunks, slot...]
    mul x0 -> x1, other arithmetic: none -> 3.05 us  [on_device(): return unit * out_gain]
    transpose x1 -> x0, local copies, waits for them, and re-layouts: 1.31 us -> none  [on_device(): weights = jnp.transpose(weights, (1, 0, 2))]
    convert_element_type x1 -> x0, other arithmetic: 1.28 us -> none  [on_device(): gain = out_gain.reshape(chunks, 1, pairs * 2 * DV).astype(jnp.float32)]
where the time goes in v2:
time: 53.6 us; the launch traced here: 53.4 us
  Pallas kernels  50.4 us (94%)
  other arithmetic  3.05 us (6%)
    pallas_call x1, Pallas kernels, on_device(): pl.pallas_call(functools.partial(kernel, inner_bits, levels, chunks, slot...  50.4 us
    mul x1, other arithmetic, on_device(): return unit * out_gain  3.05 us

profile of v2, /device:TPU:0, one launch (start us, length us, event | category | flops | bytes accessed | tf_op | source)
XLA Modules:
  0.0 53.4 jit_solution(813376454269668782)
XLA Ops:
  0.0 0.0 copy-start
  0.0 50.4 %shard_map.55 = bf16[512,2048]{1,0:T(8,128)(2,1)} custom-call(bf16[512,4096]{1,0:T(8,128)(2,1)} %q_hbm.1, bf16[512,4096]{1,0:T(8,128)(2,1)} %k_hbm.1, bf16[512,2048]{1,0:T(8,128)(2,1)} %v_hbm.1, bf16[480,512]{1,0:T(8,128)(2,1)} %bitcast.3), custom_call_target="tpu_custom_call" | custom-call | tf_op jit(solution)/shard_map/pallas_call | solution.py:267
  50.4 0.0 copy-done
  50.4 3.0 %broadcast_multiply_fusion = bf16[512,2048]{1,0:T(8,128)(2,1)} fusion(bf16[512,2048]{1,0:T(8,128)(2,1)} %shard_map.55, bf16[2048]{0:T(1024)(128)(2,1)S(1)} %copy-done), kind=kLoop, calls=%fused_computation | loop fusion | flops 1048576 | bytes 4198400 | tf_op jit(solution)/shard_map/mul | solution.py:295
Async XLA Ops:
  0.0 50.4 %copy-start = (bf16[2048]{0:T(1024)(128)(2,1)S(1)}, bf16[2048]{0:T(1024)(128)(2,1)}, u32[]{:S(2)}) copy-start(bf16[2048]{0:T(1024)(128)(2,1)} %param.9) | copy-start | bytes 12292

commit v3 on v2

--- a/solution.py
+++ b/solution.py
@@ -15,6 +15,9 @@
 ROWS = 256
 OWNED = 1
 NEAR = 3
+SIDE_GAP = 2
+FIRST = 1
+LAST_GAP = 1
 VMEM_MIB = 56
 NEAR_GAP = 2
 FAR_GAP = 2
@@ -33,7 +36,7 @@
     inner_bits, levels, chunks, slots, zero_slot, heads,
     q_hbm, k_hbm, v_hbm, w_hbm, out_hbm,
     qb, kb, vb, wt, wb, acc, ob, st, lvl, car, table,
-    in_sem, out_sem, send_sem, recv_sem, pass_send, pass_recv,
+    in_sem, out_sem, send_sem, recv_sem, pass_send, pass_recv, side_send, side_recv,
 ):
     inner, outer = lax.axis_index("sb"), lax.axis_index("sa")
     length = qb.shape[1]
@@ -65,15 +68,25 @@
         return pltpu.make_async_copy(ob.at[c], out_hbm.at[:, columns], out_sem.at[c])
 
     mine = pl.ds(core * OWNED, OWNED)
+    top = levels - 1
+    half = pl.ds(bit(1) * DV, DV)
 
     def exchange(j, c):
         if j == 0:
             source, target = st.at[c], lvl.at[0, c]
+        elif j == top:
+            source, target = car.at[j - 1, c, :, half], lvl.at[j, c, mine, half]
         else:
             source, target = car.at[j - 1, c], lvl.at[j, c, mine]
         return pltpu.make_async_remote_copy(
             src_ref=source, dst_ref=target, send_sem=send_sem.at[j, c],
             recv_sem=recv_sem.at[j, c], device_id=partner(j), device_id_type=MESH,
+        )
+
+    def across(c):
+        return pltpu.make_async_remote_copy(
+            src_ref=lvl.at[top, c, mine, half], dst_ref=lvl.at[top, c, mine, half], send_sem=side_send.at[c],
+            recv_sem=side_recv.at[c], device_id=partner(1), device_id_type=MESH,
         )
 
     def pass_on(j, c):
@@ -193,10 +206,11 @@
                 )
                 ob[c, start : start + ROWS, p * LANES : (p + 1) * LANES] = (total * scale).astype(jnp.bfloat16)
 
-    arrival = [1]
+    arrival = [FIRST]
     for j in range(1, levels):
         arrival.append(arrival[-1] + (NEAR_GAP if j < NEAR else FAR_GAP))
-    last = arrival[-1] + 1
+    crossed = arrival[-1] + SIDE_GAP
+    last = crossed + LAST_GAP
 
     @pl.loop(0, chunks + last)
     def _(tick):
@@ -213,13 +227,20 @@
             @pl.when((c >= 0) & (c < chunks))
             def _(j=j, c=c):
                 exchange(j, c).wait_recv()
-                if j > 0:
+                if j == top:
+                    across(c).start()
+                elif j > 0:
                     pass_on(j, c).start()
                 if j + 1 < levels:
                     own = st[c, mine] if j == 0 else car[j - 1, c]
                     car[j, c] = own + lvl[j, c, mine]
                     exchange(j + 1, c).start()
 
+        @pl.when((tick >= crossed) & (tick < crossed + chunks))
+        def _():
+            across(tick - crossed).wait_recv()
+            pass_on(top, tick - crossed).start()
+
         @pl.when(tick == 0)
         def _():
             weights_copy.wait()
@@ -246,6 +267,7 @@
     @pl.loop(0, chunks)
     def _(c):
         put(c).wait()
+        across(c).wait_send()
         for j in range(levels):
             exchange(j, c).wait_send()
             if j > 0:
@@ -287,6 +309,8 @@
             dma((levels, chunks)),
             dma((levels, chunks)),
             dma((levels, chunks)),
+            dma((chunks,)),
+            dma((chunks,)),
         ],
         compiler_params=pltpu.CompilerParams(
             collective_id=0, has_side_effects=True, vmem_limit_bytes=VMEM_MIB * 1024 * 1024

time: 53.6 us -> 49.9 us (0.931)
  Pallas kernels: 50.4 us -> 46.7 us
    pallas_call x1, Pallas kernels: 50.4 us -> 46.7 us  [on_device(): pl.pallas_call(functools.partial(kernel, inner_bits, levels, chunks, slot...]
where the time goes in v3:
time: 49.9 us; the launch traced here: 49.8 us
  Pallas kernels  46.7 us (94%)
  other arithmetic  3.05 us (6%)
    pallas_call x1, Pallas kernels, on_device(): pl.pallas_call(functools.partial(kernel, inner_bits, levels, chunks, slot...  46.7 us
    mul x1, other arithmetic, on_device(): return unit * out_gain  3.05 us

profile of v3, /device:TPU:0, one launch (start us, length us, event | category | flops | bytes accessed | tf_op | source)
XLA Modules:
  0.0 49.8 jit_solution(14348001010817952912)
XLA Ops:
  0.0 0.0 copy-start
  0.0 46.7 %shard_map.55 = bf16[512,2048]{1,0:T(8,128)(2,1)} custom-call(bf16[512,4096]{1,0:T(8,128)(2,1)} %q_hbm.1, bf16[512,4096]{1,0:T(8,128)(2,1)} %k_hbm.1, bf16[512,2048]{1,0:T(8,128)(2,1)} %v_hbm.1, bf16[480,512]{1,0:T(8,128)(2,1)} %bitcast.3), custom_call_target="tpu_custom_call" | custom-call | tf_op jit(solution)/shard_map/pallas_call | solution.py:289
  46.7 0.0 copy-done
  46.7 3.0 %broadcast_multiply_fusion = bf16[512,2048]{1,0:T(8,128)(2,1)} fusion(bf16[512,2048]{1,0:T(8,128)(2,1)} %shard_map.55, bf16[2048]{0:T(1024)(128)(2,1)S(1)} %copy-done), kind=kLoop, calls=%fused_computation | loop fusion | flops 1048576 | bytes 4198400 | tf_op jit(solution)/shard_map/mul | solution.py:319
Async XLA Ops:
  0.0 46.7 %copy-start = (bf16[2048]{0:T(1024)(128)(2,1)S(1)}, bf16[2048]{0:T(1024)(128)(2,1)}, u32[]{:S(2)}) copy-start(bf16[2048]{0:T(1024)(128)(2,1)} %param.9) | copy-start | bytes 12292
